TPU v7x, 256 devices: a whole 4x4x8 slice. The times are simulated.
256 devices in a mesh: seq: 32 (over x, y, core), head: 8 (over z).
Axes of the slice: x: 4, y: 4, z: 8, core: 2. Of those that a mesh axis runs over, the one named last changes fastest.
Arguments:
- tokens: bfloat16 [32768, 2048], P('seq'), may hold values from -6 to 6
- norm_gain: bfloat16 [2048], replicated, may hold values from 0.099609375 to 1.8984375
- w_qkv: bfloat16 [3, 2048, 2048], P(None, None, 'head'), may hold values from -0.176776695 to 0.176776695
- mem_gate: float32 [16], P('head'), may hold values from -3 to 3
- w_out: bfloat16 [2048, 2048], P('head'), may hold values from -0.1875 to 0.1875
Outputs:
- attended: bfloat16 [32768, 2048], P('seq', 'head')
- memory_state: float32 [32, 16, 128, 128], P('seq', 'head')
All inputs are finite; a program needn't handle non-finite values.
Results may differ from a plain program's by a relative error of at most 0.01.
The roundings to bfloat16 on the way count: a program that leaves them out, or rounds other values in their place, can miss the bound.
Values may be sent and summed in bfloat16 or wider, within the bound.
A program may use at most 64 MiB of HBM per device.

v0:
```python
import jax
import jax.numpy as jnp
from jax import lax
from jax.sharding import PartitionSpec as P

HDIM = 128


def sent_together(arrays, axis, dim, along):
    columns = [a.reshape(*a.shape[:along], -1) for a in arrays]
    both = jnp.concatenate(columns, axis=along)
    result, at, gathered = (lax.all_gather(both, axis, axis=dim, tiled=True), 0, [])
    for a, column in zip(arrays, columns):
        section = result[..., at : at + column.shape[along]]
        gathered.append(section.reshape(*section.shape[:along], *a.shape[along:]))
        at += column.shape[along]
    return tuple(gathered)


def elu_one(values_in):
    return jnp.where(values_in > 0, values_in + 1.0, jnp.exp(jnp.minimum(values_in, 0.0)))


def on_device(tokens, norm_gain, w_qkv, mem_gate, w_out):
    seg_len = tokens.shape[0]
    local_heads = w_qkv.shape[2] // HDIM
    float_tokens = tokens.astype(jnp.float32)
    normed = (
        float_tokens
        * lax.rsqrt(jnp.mean(float_tokens * float_tokens, axis=-1, keepdims=True) + 1e-05)
        * norm_gain.astype(jnp.float32)
    ).astype(jnp.bfloat16)
    projected = jnp.einsum("td,cdh->cth", normed, w_qkv, preferred_element_type=jnp.float32).astype(
        jnp.bfloat16
    )
    queries = projected[0].reshape(seg_len, local_heads, HDIM)
    key_rows = projected[1].reshape(seg_len, local_heads, HDIM)
    value_rows = projected[2].reshape(seg_len, local_heads, HDIM)
    sig_keys = elu_one(key_rows.astype(jnp.float32))
    memory_delta = jnp.einsum("thd,the->hde", sig_keys, value_rows.astype(jnp.float32))
    delta_norm = jnp.sum(sig_keys, axis=0)
    zero_memory = jnp.zeros_like(memory_delta)
    zero_norm = jnp.zeros_like(delta_norm)
    my_index = lax.axis_index("seq")
    pieces = tuple(
        (
            part.astype(jnp.float32)
            for part in sent_together(
                (memory_delta[None].astype(jnp.bfloat16), delta_norm[None].astype(jnp.bfloat16)),
                "seq",
                0,
                3,
            )
        )
    )
    row_count = pieces[0].shape[0]
    keep_rows = (jnp.arange(row_count, dtype=jnp.int32) < my_index).astype(jnp.float32)
    memory_prev = zero_memory + jnp.sum(pieces[0] * keep_rows[:, None, None, None], axis=0)
    norm_prev = zero_norm + jnp.sum(pieces[1] * keep_rows[:, None, None], axis=0)
    inv_sqrt = 1.0 / HDIM**0.5
    scores = (
        jnp.einsum("qhd,khd->hqk", queries, key_rows, preferred_element_type=jnp.float32) * inv_sqrt
    )
    row_ids = lax.broadcasted_iota(jnp.int32, (seg_len, seg_len), 0)
    col_ids = lax.broadcasted_iota(jnp.int32, (seg_len, seg_len), 1)
    scores = jnp.where((col_ids <= row_ids)[None], scores, -1e30)
    weights = jax.nn.softmax(scores, axis=-1).astype(jnp.bfloat16)
    local_out = jnp.einsum("hqk,khd->qhd", weights, value_rows, preferred_element_type=jnp.float32)
    sig_q = elu_one(queries.astype(jnp.float32))
    retrieved = jnp.einsum("thd,hde->the", sig_q, memory_prev)
    normalizer = 1.0 + jnp.einsum("thd,hd->th", sig_q, norm_prev)
    gate_share = jax.nn.sigmoid(mem_gate)[None, :, None]
    mixed_out = (
        gate_share * retrieved / normalizer[..., None] + (1.0 - gate_share) * local_out
    ).astype(jnp.bfloat16)
    mixed_out = mixed_out.reshape(seg_len, local_heads * HDIM)
    weight_cols = lax.all_to_all(w_out, "head", split_axis=1, concat_axis=0, tiled=True)
    attended = jnp.dot(
        lax.all_gather(mixed_out, "head", axis=1, tiled=True),
        weight_cols,
        preferred_element_type=jnp.float32,
    ).astype(jnp.bfloat16)
    memory_state = ((memory_prev + memory_delta) / seg_len)[None]
    return (attended, memory_state)


def solution(mesh):
    placed = (P("seq", None), P(), P(None, None, "head"), P("head"), P("head", None))
    return jax.shard_map(
        on_device,
        mesh=mesh,
        in_specs=placed,
        out_specs=(P("seq", "head"), P("seq", "head", None, None)),
        check_vma=False,
    )
```

profile of v0, /device:TPU:1, one launch (start us, length us, event | category | flops | bytes accessed | tf_op | source)
XLA Modules:
  0.0 170.5 jit_solution(17933472047963940664)
XLA Ops:
  7.2 0.0 copy-start
  7.2 0.0 copy-start.2
  7.2 0.0 all-gather.3.cloned.1.call-start
  7.2 0.0 copy-start.1
  7.2 3.2 %fusion.1 = f32[1024]{0:T(1024)S(1)} fusion(bf16[1024,2048]{1,0:T(8,128)(2,1)} %param.5), kind=kLoop, calls=%fused_computation.3 | loop fusion | flops 6290432 | bytes 4198400 | tf_op jit(solution)/shard_map/reduce_sum | solution.py:30
  10.5 1.1 copy-done.1
  11.6 3.9 %fusion.17 = bf16[3,1024,256]{1,2,0:T(8,128)(2,1)S(1)} fusion(bf16[3,2048,256]{2,1,0:T(8,128)(2,1)S(1)} %copy-done, bf16[1024,2048]{1,0:T(8,128)(2,1)S(1)} %copy-done.1, f32[2048]{0:T(1024)S(1)} %convert_element_type.76, f32[1024]{0:T(1024)S(1)} %add_rsqrt_fusion), kind=kOutput, calls=%fused_computation.30 | convolution fusion | flops 3230400512 | bytes 8925184 | tf_op jit(solution)/shard_map/td,cdh->cth/dot_general | solution.py:33
  15.5 0.0 copy-start.3
  15.5 1.2 fusion.58
  16.7 0.4 fusion.32
  17.0 2.1 %copy.44 = bf16[1024,2,128]{2,0,1:T(8,128)(2,1)} copy(bf16[1024,2,128]{0,2,1:T(8,128)(2,1)} %bitcast.59) | data formatting | bytes 1048576 | tf_op jit(solution)/shard_map/reshape;squeeze | solution.py:37
  19.1 1.6 fusion.27
  20.8 0.7 copy.46
  21.4 0.0 all-gather.3.cloned.1.call-update
  21.5 0.2 all-gather.5.cloned.1.call-start
  21.7 2.1 %copy.47 = bf16[1024,2,128]{2,0,1:T(8,128)(2,1)} copy(bf16[1024,2,128]{0,2,1:T(8,128)(2,1)} %bitcast.61) | data formatting | bytes 1048576 | tf_op jit(solution)/shard_map/reshape;squeeze | solution.py:36
  23.8 1.3 iota_compare_fusion
  25.0 0.0 copy-done.3
  25.1 8.2 %fusion.59 = (f32[2,1024]{1,0:T(2,128)S(1)}, f32[2,1024,1024]{1,2,0:T(8,128)}) fusion(pred[1024,1024]{0,1:T(8,128)(4,1)} %iota_compare_fusion, bf16[1024,2,128]{0,2,1:T(8,128)(2,1)} %bitcast.62, bf16[1024,2,128]{0,2,1:T(8,128)(2,1)} %bitcast.60), kind=kOutput, calls=%fused_computation.78 | convolution fusion | flops 545260544 | bytes 10493952 | tf_op jit(solution)/shard_map/sub | solution.py:67
  33.2 5.3 %fusion.24 = f32[1024,2,128]{0,2,1:T(8,128)} fusion(bf16[1024,2,128]{0,2,1:T(8,128)(2,1)} %bitcast.66, f32[2,1024,1024]{1,2,0:T(8,128)} %get-tuple-element.18, f32[2,1024]{1,0:T(2,128)S(1)} %get-tuple-element.17, f32[2]{0:T(128)S(1)} %get-tuple-element.12), kind=kOutput, calls=%fused_computation.36 | convolution fusion | flops 541327360 | bytes 9969672 | tf_op jit(solution)/shard_map/hqk,khd->qhd/dot_general | solution.py:68
  38.5 36.3 %all-gather.3.cloned.1.call-done = bf16[32,2,128,129]{2,1,3,0:T(2,128)(2,1)} async-done(((bf16[1,2,128,129]{2,1,3,0:T(2,128)(2,1)}), bf16[32,2,128,129]{2,1,3,0:T(2,128)(2,1)}) %all-gather.3.cloned.1.call-update) | async-done | bytes 2113552 | tf_op jit(solution)/shard_map/all_gather | solution.py:12
  74.8 0.8 fusion.48
  75.6 1.4 fusion.36
  77.0 3.9 %multiply_reduce_fusion = f32[2,128,128]{1,0,2:T(2,128)S(1)} fusion(f32[32]{0:T(128)S(1)} %compare_convert_fusion, bf16[32,2,128,129]{2,1,3,0:T(2,128)(2,1)} %all-gather.3.cloned.1.call-done), kind=kLoop, calls=%fused_computation.15 | loop fusion | flops 3112960 | bytes 2228352 | tf_op jit(solution)/shard_map/reduce_sum | solution.py:58
  80.9 2.7 %fusion.25 = bf16[1024,2,128]{0,2,1:T(8,128)(2,1)} fusion(f32[1024,2,128]{0,2,1:T(8,128)} %fusion.24, bf16[1024,2,128]{2,0,1:T(8,128)(2,1)} %copy.47, f32[1024,2]{0,1:T(2,128)S(1)} %fusion.49, f32[2]{0:T(128)S(1)} %get-tuple-element.13, f32[2,128,128]{1,0,2:T(2,128)S(1)} %multiply_reduce_fusion), kind=kOutput, calls=%fused_computation.37 | convolution fusion | flops 69468160 | bytes 2236424 | tf_op jit(solution)/shard_map/thd,hde->the/dot_general | solution.py:70
  83.6 0.0 all-gather.5.cloned.1.call-update
  83.6 2.3 %copy.52 = bf16[256,2048]{0,1:T(8,128)(2,1)} copy(bf16[256,2048]{1,0:T(8,128)(2,1)} %param.9) | data formatting | bytes 2097152 | tf_op args[4]
  85.9 46.3 %all_to_all.19 = bf16[256,8,256]{0,2,1:T(8,128)(2,1)} all-to-all(bf16[256,8,256]{0,2,1:T(8,128)(2,1)} %bitcast.58), channel_id=1, replica_groups=mesh['seq'=32,'head'=8] {'head'}, dimensions={1} | all-to-all | bytes 2097152 | tf_op jit(solution)/shard_map/all_to_all | solution.py:77
  132.2 2.3 %copy.53 = bf16[8,256,256]{2,1,0:T(8,128)(2,1)} copy(bf16[8,256,256]{1,2,0:T(8,128)(2,1)} %bitcast.57) | data formatting | bytes 2097152 | tf_op jit(solution)/shard_map/all_to_all | solution.py:77
  134.6 0.8 copy.55
  135.3 23.8 %all-gather.5.cloned.1.call-done = bf16[1024,2048]{0,1:T(8,128)(2,1)} async-done(((bf16[1024,256]{0,1:T(8,128)(2,1)}), bf16[1024,2048]{0,1:T(8,128)(2,1)}) %all-gather.5.cloned.1.call-update) | async-done | bytes 4194320 | tf_op jit(solution)/shard_map/all_gather | solution.py:79
  159.1 4.6 %convolution_convert_fusion = bf16[1024,256]{1,0:T(8,128)(2,1)} fusion(bf16[1024,2048]{0,1:T(8,128)(2,1)} %all-gather.5.cloned.1.call-done, bf16[2048,256]{1,0:T(8,128)(2,1)} %bitcast.63), kind=kOutput, calls=%fused_computation.38 | convolution fusion | flops 1074003968 | bytes 5767168 | tf_op jit(solution)/shard_map/dot_general | solution.py:78
  (11 shorter events, 0.1 us)
Async XLA Ops:
  7.2 3.3 %copy-start = (bf16[3,2048,256]{2,1,0:T(8,128)(2,1)S(1)}, bf16[3,2048,256]{2,1,0:T(8,128)(2,1)}, u32[]{:S(2)}) copy-start(bf16[3,2048,256]{2,1,0:T(8,128)(2,1)} %param.7) | copy-start | bytes 9437188
  7.2 3.3 %copy-start.2 = (bf16[2048]{0:T(1024)(128)(2,1)S(1)}, bf16[2048]{0:T(1024)(128)(2,1)}, u32[]{:S(2)}) copy-start(bf16[2048]{0:T(1024)(128)(2,1)} %param.6) | copy-start | bytes 12292
  7.2 67.6 %all-gather.3.cloned.1.call-start = ((), (), s32[]{:S(2)}) async-start(), calls=%async_computation.1 | async-start | bytes 2179584 | tf_op jit(solution)/shard_map/all_gather | solution.py:12
  7.2 4.4 %copy-start.1 = (bf16[1024,2048]{1,0:T(8,128)(2,1)S(1)}, bf16[1024,2048]{1,0:T(8,128)(2,1)}, u32[]{:S(2)}) copy-start(bf16[1024,2048]{1,0:T(8,128)(2,1)} %param.5) | copy-start | bytes 12582916
  15.5 9.6 %copy-start.3 = (f32[2]{0:T(128)S(1)}, f32[2]{0:T(128)}, u32[]{:S(2)}) copy-start(f32[2]{0:T(128)} %param.8) | copy-start | bytes 28
  21.5 137.7 %all-gather.5.cloned.1.call-start = ((), (), s32[]{:S(2)}) async-start(), calls=%async_computation.2 | async-start | bytes 4718592 | tf_op jit(solution)/shard_map/all_gather | solution.py:79
Sparse Core Ops, SparseCore 0:
  21.6 53.1 all-gather.2
  83.7 75.3 all-gather.4
where the time goes:
time: 171 us
  waiting for transfers between devices  60.1 us (35%)
  blocking collectives  46.3 us (27%)
  matrix products  27.6 us (16%)
  between operations  14.2 us (8%)
  local copies, waits for them, and re-layouts  12.4 us (7%)
  other arithmetic  9.68 us (6%)
    all_to_all x1, blocking collectives, on_device(): lax.all_to_all(w_out, 'head', split_axis=1, concat_axis=0, tiled=True)  46.3 us
    all_gather x1, waiting for transfers between devices, sent_together(): lax.all_gather(both, axis, axis=dim, tiled=True)  36.3 us
    all_gather x1, waiting for transfers between devices, on_device(): lax.all_gather(mixed_out, 'head', axis=1, tiled=True)  23.8 us
    sub x1, matrix products, on_device(): weights = jax.nn.softmax(scores, axis=-1).astype(jnp.bfloat16)  8.15 us
    dot_general x1, matrix products, on_device(): jnp.einsum('hqk,khd->qhd', weights, value_rows, preferred_element_type=jn...  5.3 us
    dot_general x1, matrix products, on_device(): jnp.dot(lax.all_gather(mixed_out, 'head', axis=1, tiled=True), weight_col...  4.57 us
    unnamed x10, local copies, waits for them, and re-layouts  4.15 us
    reduce_sum x1, other arithmetic, on_device(): jnp.sum(pieces[0] * keep_rows[:, None, None, None], axis=0)  3.93 us
  transfers between devices with their start and end apart: 2, of which 2 were waited for; matrix products, arithmetic and copies ran while one was open for 13% of the time, Pallas kernels for 0%

commit v1 on v0

--- a/solution.py
+++ b/solution.py
@@ -4,6 +4,22 @@
 from jax.sharding import PartitionSpec as P
 
 HDIM = 128
+
+
+def gather_around(x, axis, dim):
+    ways, here, step = (lax.axis_size(axis), lax.axis_index(axis), x.shape[dim])
+    dims = [n * ways if d == dim else n for d, n in enumerate(x.shape)]
+    full = lax.dynamic_update_slice_in_dim(jnp.zeros(dims, x.dtype), x, here * step, axis=dim)
+    going_up = going_down = x
+    for far in range(1, ways // 2 + 1):
+        going_up = lax.ppermute(going_up, axis, [(d, (d + 1) % ways) for d in range(ways)])
+        full = lax.dynamic_update_slice_in_dim(full, going_up, (here - far) % ways * step, axis=dim)
+        if 2 * far < ways:
+            going_down = lax.ppermute(going_down, axis, [(d, (d - 1) % ways) for d in range(ways)])
+            full = lax.dynamic_update_slice_in_dim(
+                full, going_down, (here + far) % ways * step, axis=dim
+            )
+    return full
 
 
 def sent_together(arrays, axis, dim, along):
@@ -76,9 +92,7 @@
     mixed_out = mixed_out.reshape(seg_len, local_heads * HDIM)
     weight_cols = lax.all_to_all(w_out, "head", split_axis=1, concat_axis=0, tiled=True)
     attended = jnp.dot(
-        lax.all_gather(mixed_out, "head", axis=1, tiled=True),
-        weight_cols,
-        preferred_element_type=jnp.float32,
+        gather_around(mixed_out, "head", 1), weight_cols, preferred_element_type=jnp.float32
     ).astype(jnp.bfloat16)
     memory_state = ((memory_prev + memory_delta) / seg_len)[None]
     return (attended, memory_state)

time: 171 us -> 150 us (0.88); the launches traced: 171 us -> 148 us
  blocking collectives: 46.3 us -> 0 us
  starting transfers between devices: 0.26 us -> 17.7 us
  local copies, waits for them, and re-layouts: 12.4 us -> 18.7 us
  matrix products: 27.6 us -> 24.5 us
  waiting for transfers between devices: 60.1 us -> 62.7 us
    all_to_all x1 -> x0, blocking collectives: 46.3 us -> none  [on_device(): lax.all_to_all(w_out, 'head', split_axis=1, concat_axis=0, tiled=True)]
    ppermute x0 -> x7, waiting for transfers between devices: none -> 37.7 us  [the longest x4 37.7 us: gather_around(): lax.ppermute(going_up, axis, [(d, (d + 1) % ways) for d in range(ways)])]
    all_gather x1 -> x0, waiting for transfers between devices: 23.8 us -> none  [on_device(): lax.all_gather(mixed_out, 'head', axis=1, tiled=True)]
    all_gather x1, waiting for transfers between devices: 36.3 us -> 25 us  [sent_together(): lax.all_gather(both, axis, axis=dim, tiled=True)]
    all_to_all x0 -> x1, starting transfers between devices: none -> 9.01 us  [on_device(): lax.all_to_all(w_out, 'head', split_axis=1, concat_axis=0, tiled=True)]
    ppermute x0 -> x7, starting transfers between devices: none -> 8.63 us  [the longest x3 7.27 us: gather_around(): lax.ppermute(going_down, axis, [(d, (d - 1) % ways) for d in range(ways)])]
    dynamic_update_slice x0 -> x8, local copies, waits for them, and re-layouts: none -> 4.49 us  [the longest x4 2.25 us: gather_around(): lax.dynamic_update_slice_in_dim(full, going_up, (here - far) % ways * ste...]
    dot_general x1, matrix products: 4.57 us -> 2.12 us  [on_device(): jnp.dot(gather_around(mixed_out, 'head', 1), weight_cols, preferred_eleme...]
  transfers between devices with their start and end apart: 2 -> 9, of which waited for: 2 -> 5; matrix products, arithmetic and copies ran while one was open for 13% -> 24% of each run, Pallas kernels for 0% -> 0%
where the time goes in v1:
time: 150 us; the launch traced here: 148 us
  waiting for transfers between devices  62.7 us (42%)
  matrix products  24.5 us (16%)
  local copies, waits for them, and re-layouts  18.7 us (12%)
  starting transfers between devices  17.7 us (12%)
  between operations  14.2 us (9%)
  other arithmetic  9.73 us (6%)
    ppermute x4, waiting for transfers between devices, gather_around(): lax.ppermute(going_up, axis, [(d, (d + 1) % ways) for d in range(ways)])  37.7 us
    all_gather x1, waiting for transfers between devices, sent_together(): lax.all_gather(both, axis, axis=dim, tiled=True)  25 us
    all_to_all x1, starting transfers between devices, on_device(): lax.all_to_all(w_out, 'head', split_axis=1, concat_axis=0, tiled=True)  9.01 us
    sub x1, matrix products, on_device(): weights = jax.nn.softmax(scores, axis=-1).astype(jnp.bfloat16)  8.17 us
    ppermute x3, starting transfers between devices, gather_around(): lax.ppermute(going_down, axis, [(d, (d - 1) % ways) for d in range(ways)])  7.27 us
    unnamed x20, local copies, waits for them, and re-layouts  5.46 us
    dot_general x1, matrix products, on_device(): jnp.einsum('hqk,khd->qhd', weights, value_rows, preferred_element_type=jn...  5.38 us
    reduce_sum x1, other arithmetic, on_device(): jnp.sum(pieces[0] * keep_rows[:, None, None, None], axis=0)  3.93 us
  transfers between devices with their start and end apart: 9, of which 5 were waited for; matrix products, arithmetic and copies ran while one was open for 24% of the time, Pallas kernels for 0%

profile of v1, /device:TPU:1, one launch (start us, length us, event | category | flops | bytes accessed | tf_op | source)
XLA Modules:
  0.0 147.5 jit_solution(1892316061743600234)
XLA Ops:
  7.2 3.2 %fusion.1 = f32[1024]{0:T(1024)S(1)} fusion(bf16[1024,2048]{1,0:T(8,128)(2,1)} %param.5), kind=kLoop, calls=%fused_computation.3 | loop fusion | flops 6290432 | bytes 4198400 | tf_op jit(solution)/shard_map/reduce_sum | solution.py:46
  10.5 1.1 copy-done.1
  11.6 3.9 %fusion.17 = bf16[3,1024,256]{1,2,0:T(8,128)(2,1)S(1)} fusion(bf16[3,2048,256]{2,1,0:T(8,128)(2,1)S(1)} %copy-done, bf16[1024,2048]{1,0:T(8,128)(2,1)S(1)} %copy-done.1, f32[2048]{0:T(1024)S(1)} %convert_element_type.76, f32[1024]{0:T(1024)S(1)} %add_rsqrt_fusion), kind=kOutput, calls=%fused_computation.30 | convolution fusion | flops 3230400512 | bytes 8925184 | tf_op jit(solution)/shard_map/td,cdh->cth/dot_general | solution.py:49
  15.5 1.2 fusion.58
  17.0 2.0 %copy.44 = bf16[1024,2,128]{2,0,1:T(8,128)(2,1)} copy(bf16[1024,2,128]{0,2,1:T(8,128)(2,1)} %bitcast.58) | data formatting | bytes 1048576 | tf_op jit(solution)/shard_map/reshape;squeeze | solution.py:53
  19.0 1.6 %fusion.27 = f32[2,128,128]{1,2,0:T(8,128)S(1)} fusion(bf16[1024,2,128]{0,2,1:T(8,128)(2,1)} %bitcast.66, bf16[1024,2,128]{2,0,1:T(8,128)(2,1)} %copy.44), kind=kOutput, calls=%fused_computation.40 | convolution fusion | flops 68419584 | bytes 1179648 | tf_op jit(solution)/shard_map/thd,the->hde/dot_general | solution.py:56
  21.5 2.3 %copy.52 = bf16[256,2048]{0,1:T(8,128)(2,1)} copy(bf16[256,2048]{1,0:T(8,128)(2,1)} %param.9) | data formatting | bytes 2097152 | tf_op args[4]
  23.7 9.0 %all-to-all-start = ((bf16[256,8,256]{0,2,1:T(8,128)(2,1)}), bf16[256,8,256]{0,2,1:T(8,128)(2,1)}, u32[]{:S(2)}, u32[]{:S(2)}) async-start(bf16[256,8,256]{0,2,1:T(8,128)(2,1)} %bitcast.57), calls=%async_computation | async-start | bytes 2097152 | tf_op jit(solution)/shard_map/all_to_all | solution.py:93
  32.7 2.0 %copy.47 = bf16[1024,2,128]{2,0,1:T(8,128)(2,1)} copy(bf16[1024,2,128]{0,2,1:T(8,128)(2,1)} %bitcast.60) | data formatting | bytes 1048576 | tf_op jit(solution)/shard_map/reshape;squeeze | solution.py:52
  34.8 1.3 iota_compare_fusion
  36.1 8.2 %fusion.59 = (f32[2,1024]{1,0:T(2,128)S(1)}, f32[2,1024,1024]{1,2,0:T(8,128)}) fusion(pred[1024,1024]{0,1:T(8,128)(4,1)} %iota_compare_fusion, bf16[1024,2,128]{0,2,1:T(8,128)(2,1)} %bitcast.61, bf16[1024,2,128]{0,2,1:T(8,128)(2,1)} %bitcast.59), kind=kOutput, calls=%fused_computation.86 | convolution fusion | flops 545260544 | bytes 10493952 | tf_op jit(solution)/shard_map/sub | solution.py:83
  44.3 5.4 %fusion.24 = f32[1024,2,128]{0,2,1:T(8,128)} fusion(bf16[1024,2,128]{0,2,1:T(8,128)(2,1)} %bitcast.67, f32[2,1024,1024]{1,2,0:T(8,128)} %get-tuple-element.18, f32[2,1024]{1,0:T(2,128)S(1)} %get-tuple-element.17, f32[2]{0:T(128)S(1)} %get-tuple-element.12), kind=kOutput, calls=%fused_computation.36 | convolution fusion | flops 541327360 | bytes 9969672 | tf_op jit(solution)/shard_map/hqk,khd->qhd/dot_general | solution.py:84
  49.7 25.0 %all-gather.2.cloned.1.call-done = bf16[32,2,128,129]{2,1,3,0:T(2,128)(2,1)} async-done(((bf16[1,2,128,129]{2,1,3,0:T(2,128)(2,1)}), bf16[32,2,128,129]{2,1,3,0:T(2,128)(2,1)}) %all-gather.2.cloned.1.call-update) | async-done | bytes 2113552 | tf_op jit(solution)/shard_map/all_gather | solution.py:28
  74.7 0.8 fusion.48
  75.6 1.4 fusion.36
  77.0 3.9 %multiply_reduce_fusion = f32[2,128,128]{1,0,2:T(2,128)S(1)} fusion(f32[32]{0:T(128)S(1)} %compare_convert_fusion, bf16[32,2,128,129]{2,1,3,0:T(2,128)(2,1)} %all-gather.2.cloned.1.call-done), kind=kLoop, calls=%fused_computation.15 | loop fusion | flops 3112960 | bytes 2228352 | tf_op jit(solution)/shard_map/reduce_sum | solution.py:74
  80.9 1.9 %fusion.25 = bf16[1024,2,128]{0,2,1:T(8,128)(2,1)S(1)} fusion(f32[1024,2,128]{0,2,1:T(8,128)} %fusion.24, bf16[1024,2,128]{2,0,1:T(8,128)(2,1)} %copy.47, f32[1024,2]{0,1:T(2,128)S(1)} %fusion.49, f32[2]{0:T(128)S(1)} %get-tuple-element.13, f32[2,128,128]{1,0,2:T(2,128)S(1)} %multiply_reduce_fusion), kind=kOutput, calls=%fused_computation.37 | convolution fusion | flops 69468160 | bytes 2236424 | tf_op jit(solution)/shard_map/thd,hde->the/dot_general | solution.py:86
  82.8 1.4 collective-permute-start
  84.2 1.9 %collective-permute-start.1 = (bf16[1024,256]{0,1:T(8,128)(2,1)S(1)}, bf16[1024,256]{0,1:T(8,128)(2,1)}, u32[]{:S(2)}, u32[]{:S(2)}) collective-permute-start(bf16[1024,256]{0,1:T(8,128)(2,1)S(1)} %bitcast.64), channel_id=1, source_target_pairs={{0,7},{1,0},{2,1},{3,2},{4,3},{5,4},{6,5},{7,6},{8,15},{9,8},{10,9... | collective-permute-start | bytes 1572872 | tf_op jit(solution)/shard_map/ppermute | solution.py:18
  86.0 12.0 %collective-permute-done = bf16[1024,256]{0,1:T(8,128)(2,1)S(1)} collective-permute-done((bf16[1024,256]{0,1:T(8,128)(2,1)S(1)}, bf16[1024,256]{0,1:T(8,128)(2,1)S(1)}, u32[]{:S(2)}, u32[]{:S(2)}) %collective-permute-start) | collective-permute-done | bytes 524320 | tf_op jit(solution)/shard_map/ppermute | solution.py:15
  98.1 0.8 copy-done.3
  98.8 2.7 %collective-permute-start.3 = (bf16[1024,256]{0,1:T(8,128)(2,1)}, bf16[1024,256]{0,1:T(8,128)(2,1)}, u32[]{:S(2)}, u32[]{:S(2)}) collective-permute-start(bf16[1024,256]{0,1:T(8,128)(2,1)} %collective-permute-done.1), channel_id=1, source_target_pairs={{0,7},{1,0},{2,1},{3,2},{4,3},{5,4},{6,5},{7,6},{8,15},{9,8},{10,9... | collective-permute-start | bytes 1572872 | tf_op jit(solution)/shard_map/ppermute | solution.py:18
  101.5 11.3 %collective-permute-done.2 = bf16[1024,256]{0,1:T(8,128)(2,1)} collective-permute-done((bf16[1024,256]{0,1:T(8,128)(2,1)S(1)}, bf16[1024,256]{0,1:T(8,128)(2,1)}, u32[]{:S(2)}, u32[]{:S(2)}) %collective-permute-start.2) | collective-permute-done | bytes 524320 | tf_op jit(solution)/shard_map/ppermute | solution.py:15
  112.9 2.3 %copy.53 = bf16[8,256,256]{2,1,0:T(8,128)(2,1)} copy(bf16[8,256,256]{1,2,0:T(8,128)(2,1)} %bitcast.16) | data formatting | bytes 2097152 | tf_op jit(solution)/shard_map/all_to_all | solution.py:93
  117.0 2.7 %collective-permute-start.5 = (bf16[1024,256]{0,1:T(8,128)(2,1)}, bf16[1024,256]{0,1:T(8,128)(2,1)S(1)}, u32[]{:S(2)}, u32[]{:S(2)}) collective-permute-start(bf16[1024,256]{0,1:T(8,128)(2,1)} %collective-permute-done.3), channel_id=1, source_target_pairs={{0,7},{1,0},{2,1},{3,2},{4,3},{5,4},{6,5},{7,6},{8,15},{9,8},{10,9... | collective-permute-start | bytes 1572872 | tf_op jit(solution)/shard_map/ppermute | solution.py:18
  119.8 6.4 %collective-permute-done.4 = bf16[1024,256]{0,1:T(8,128)(2,1)} collective-permute-done((bf16[1024,256]{0,1:T(8,128)(2,1)}, bf16[1024,256]{0,1:T(8,128)(2,1)}, u32[]{:S(2)}, u32[]{:S(2)}) %collective-permute-start.4) | collective-permute-done | bytes 524320 | tf_op jit(solution)/shard_map/ppermute | solution.py:15
  126.2 1.1 constant_dynamic-update-slice_fusion.5
  127.3 1.1 constant_dynamic-update-slice_fusion.4
  128.4 1.1 constant_dynamic-update-slice_fusion.3
  129.5 1.1 constant_dynamic-update-slice_fusion.2
  130.6 7.9 %collective-permute-done.6 = bf16[1024,256]{0,1:T(8,128)(2,1)S(1)} collective-permute-done((bf16[1024,256]{0,1:T(8,128)(2,1)}, bf16[1024,256]{0,1:T(8,128)(2,1)S(1)}, u32[]{:S(2)}, u32[]{:S(2)}) %collective-permute-start.6) | collective-permute-done | bytes 524320 | tf_op jit(solution)/shard_map/ppermute | solution.py:15
  138.6 2.1 %convolution_convert_fusion = bf16[1024,256]{1,0:T(8,128)(2,1)} fusion(bf16[1024,2048]{0,1:T(8,128)(2,1)S(1)} %constant_dynamic-update-slice_fusion, bf16[2048,256]{1,0:T(8,128)(2,1)S(1)} %bitcast.62), kind=kOutput, calls=%fused_computation.38 | convolution fusion | flops 1074003968 | bytes 5767168 | tf_op jit(solution)/shard_map/dot_general | solution.py:94
  (42 shorter events, 3.2 us)
Async XLA Ops:
  7.2 3.3 %copy-start = (bf16[3,2048,256]{2,1,0:T(8,128)(2,1)S(1)}, bf16[3,2048,256]{2,1,0:T(8,128)(2,1)}, u32[]{:S(2)}) copy-start(bf16[3,2048,256]{2,1,0:T(8,128)(2,1)} %param.7) | copy-start | bytes 9437188
  7.2 3.3 %copy-start.7 = (bf16[2048]{0:T(1024)(128)(2,1)S(1)}, bf16[2048]{0:T(1024)(128)(2,1)}, u32[]{:S(2)}) copy-start(bf16[2048]{0:T(1024)(128)(2,1)} %param.6) | copy-start | bytes 12292
  7.2 67.6 %all-gather.2.cloned.1.call-start = ((), (), s32[]{:S(2)}) async-start(), calls=%async_computation.1 | async-start | bytes 2179584 | tf_op jit(solution)/shard_map/all_gather | solution.py:28
  7.2 4.4 %copy-start.1 = (bf16[1024,2048]{1,0:T(8,128)(2,1)S(1)}, bf16[1024,2048]{1,0:T(8,128)(2,1)}, u32[]{:S(2)}) copy-start(bf16[1024,2048]{1,0:T(8,128)(2,1)} %param.5) | copy-start | bytes 12582916
  19.0 17.1 %copy-start.8 = (f32[2]{0:T(128)S(1)}, f32[2]{0:T(128)}, u32[]{:S(2)}) copy-start(f32[2]{0:T(128)} %param.8) | copy-start | bytes 28
  23.7 89.2 %all-to-all-start = ((bf16[256,8,256]{0,2,1:T(8,128)(2,1)}), bf16[256,8,256]{0,2,1:T(8,128)(2,1)}, u32[]{:S(2)}, u32[]{:S(2)}) async-start(bf16[256,8,256]{0,2,1:T(8,128)(2,1)} %bitcast.57), calls=%async_computation | async-start | bytes 2097152 | tf_op jit(solution)/shard_map/all_to_all | solution.py:93
  82.8 30.1 %copy-start.5 = (bf16[1024,2,128]{0,2,1:T(8,128)(2,1)}, bf16[1024,2,128]{0,2,1:T(8,128)(2,1)S(1)}, u32[]{:S(2)}) copy-start(bf16[1024,2,128]{0,2,1:T(8,128)(2,1)S(1)} %fusion.25) | copy-start | bytes 1572868
  82.8 15.2 %collective-permute-start = (bf16[1024,256]{0,1:T(8,128)(2,1)S(1)}, bf16[1024,256]{0,1:T(8,128)(2,1)S(1)}, u32[]{:S(2)}, u32[]{:S(2)}) collective-permute-start(bf16[1024,256]{0,1:T(8,128)(2,1)S(1)} %bitcast.63), channel_id=1, source_target_pairs={{0,1},{1,2},{2,3},{3,4},{4,5},{5,6},{6,7},{7,0},{8,9},{9,10},{10,1... | collective-permute-start | bytes 1572872 | tf_op jit(solution)/shard_map/ppermute | solution.py:15
  84.2 14.7 %collective-permute-start.1 = (bf16[1024,256]{0,1:T(8,128)(2,1)S(1)}, bf16[1024,256]{0,1:T(8,128)(2,1)}, u32[]{:S(2)}, u32[]{:S(2)}) collective-permute-start(bf16[1024,256]{0,1:T(8,128)(2,1)S(1)} %bitcast.64), channel_id=1, source_target_pairs={{0,7},{1,0},{2,1},{3,2},{4,3},{5,4},{6,5},{7,6},{8,15},{9,8},{10,9... | collective-permute-start | bytes 1572872 | tf_op jit(solution)/shard_map/ppermute | solution.py:18
  98.1 0.8 copy-start.3
  98.8 14.0 %collective-permute-start.2 = (bf16[1024,256]{0,1:T(8,128)(2,1)S(1)}, bf16[1024,256]{0,1:T(8,128)(2,1)}, u32[]{:S(2)}, u32[]{:S(2)}) collective-permute-start(bf16[1024,256]{0,1:T(8,128)(2,1)S(1)} %collective-permute-done), channel_id=1, source_target_pairs={{0,1},{1,2},{2,3},{3,4},{4,5},{5,6},{6,7},{7,0},{8,9},{9,10},{10,1... | collective-permute-start | bytes 1572872 | tf_op jit(solution)/shard_map/ppermute | solution.py:15
  98.8 18.2 %collective-permute-start.3 = (bf16[1024,256]{0,1:T(8,128)(2,1)}, bf16[1024,256]{0,1:T(8,128)(2,1)}, u32[]{:S(2)}, u32[]{:S(2)}) collective-permute-start(bf16[1024,256]{0,1:T(8,128)(2,1)} %collective-permute-done.1), channel_id=1, source_target_pairs={{0,7},{1,0},{2,1},{3,2},{4,3},{5,4},{6,5},{7,6},{8,15},{9,8},{10,9... | collective-permute-start | bytes 1572872 | tf_op jit(solution)/shard_map/ppermute | solution.py:18
  112.9 13.3 %collective-permute-start.4 = (bf16[1024,256]{0,1:T(8,128)(2,1)}, bf16[1024,256]{0,1:T(8,128)(2,1)}, u32[]{:S(2)}, u32[]{:S(2)}) collective-permute-start(bf16[1024,256]{0,1:T(8,128)(2,1)} %collective-permute-done.2), channel_id=1, source_target_pairs={{0,1},{1,2},{2,3},{3,4},{4,5},{5,6},{6,7},{7,0},{8,9},{9,10},{10,1... | collective-permute-start | bytes 1572872 | tf_op jit(solution)/shard_map/ppermute | solution.py:15
  115.9 1.0 copy-start.6
  115.9 3.8 %copy-start.4 = (bf16[1024,256]{0,1:T(8,128)(2,1)S(1)}, bf16[1024,256]{0,1:T(8,128)(2,1)}, u32[]{:S(2)}) copy-start(bf16[1024,256]{0,1:T(8,128)(2,1)} %copy-done.3) | copy-start | bytes 1572868
  117.0 21.6 %copy-start.2 = (bf16[8,256,256]{2,1,0:T(8,128)(2,1)S(1)}, bf16[8,256,256]{2,1,0:T(8,128)(2,1)}, u32[]{:S(2)}) copy-start(bf16[8,256,256]{2,1,0:T(8,128)(2,1)} %copy.53) | copy-start | bytes 3145732
  117.0 13.5 %collective-permute-start.5 = (bf16[1024,256]{0,1:T(8,128)(2,1)}, bf16[1024,256]{0,1:T(8,128)(2,1)S(1)}, u32[]{:S(2)}, u32[]{:S(2)}) collective-permute-start(bf16[1024,256]{0,1:T(8,128)(2,1)} %collective-permute-done.3), channel_id=1, source_target_pairs={{0,7},{1,0},{2,1},{3,2},{4,3},{5,4},{6,5},{7,6},{8,15},{9,8},{10,9... | collective-permute-start | bytes 1572872 | tf_op jit(solution)/shard_map/ppermute | solution.py:18
  126.2 12.3 %collective-permute-start.6 = (bf16[1024,256]{0,1:T(8,128)(2,1)}, bf16[1024,256]{0,1:T(8,128)(2,1)S(1)}, u32[]{:S(2)}, u32[]{:S(2)}) collective-permute-start(bf16[1024,256]{0,1:T(8,128)(2,1)} %collective-permute-done.4), channel_id=1, source_target_pairs={{0,1},{1,2},{2,3},{3,4},{4,5},{5,6},{6,7},{7,0},{8,9},{9,10},{10,1... | collective-permute-start | bytes 1572872 | tf_op jit(solution)/shard_map/ppermute | solution.py:15
Sparse Core Ops, SparseCore 0:
  21.6 53.1 all-gather.1
